TPU v7x, 128 devices: a whole 4x4x4 slice. The times are simulated.
128 devices in a mesh: group: 8 (over y, core), tile: 16 (over x, z).
Axes of the slice: x: 4, y: 4, z: 4, core: 2. Of those that a mesh axis runs over, the one named last changes fastest.
Arguments:
- embeddings: bfloat16 [49152, 768], P(('group', 'tile')), may hold values from -15 to 15
- clusters: int32 [49152], P(('group', 'tile')), may hold values from 0 to 31, as said below
- cluster_owner: int32 [32], replicated, may hold values from 0 to 7, as said below
Outputs:
- neighbours: bfloat16 [49152, 768], P(('group', 'tile'))
- log_mass: float32 [49152], P(('group', 'tile'))
Inputs may be any that keep to these rules, and one draw needn't show every extreme that they name: Among the 384 rows of one device at most 72 belong to clusters of any one group; in every draw one group has exactly 72 rows on every device. `cluster_owner`: each group owns exactly 4 clusters.
All inputs are finite; a program needn't handle non-finite values.
Results may differ from a plain program's by a relative error of at most 0.034.
Values may be sent and summed in bfloat16 or wider, within the bound.
No kernel may reach another device: no remote copies, remote signals or barrier semaphores. Data moves between devices by JAX's collectives and lax.ppermute only.
A program may use at most 128 MiB of HBM per device.

v0:
```python
import math
import jax
import jax.numpy as jnp
from jax import lax
from jax.sharding import PartitionSpec as P

score_scale = 3.0
penalty = 2.0


def block_scores(queries, query_ids, key_rows, key_ids):
    feature_width = queries.shape[1]
    products = lax.dot_general(
        queries, key_rows, (((1,), (1,)), ((), ())), preferred_element_type=jnp.float32
    )
    differs = (query_ids[:, None] != key_ids[None, :]).astype(jnp.float32)
    return products * (score_scale / math.sqrt(feature_width)) - penalty * differs


def partial_terms(scores, usable, key_rows):
    row_peak = jnp.max(jnp.where(usable, scores, 0.0), axis=1)
    weights = jnp.exp(jnp.where(usable, scores - row_peak[:, None], -jnp.inf))
    row_total = jnp.sum(weights, axis=1)
    weighted = jnp.dot(weights.astype(jnp.bfloat16), key_rows, preferred_element_type=jnp.float32)
    return (row_peak, row_total, weighted)


def combine_terms(former, second):
    row_peak = jnp.maximum(former[0], second[0])
    factor_one = jnp.exp(former[0] - row_peak)
    factor_two = jnp.exp(second[0] - row_peak)
    row_total = former[1] * factor_one + second[1] * factor_two
    weighted = second[2] * factor_two[:, None]
    return (row_peak, row_total, weighted)


def per_device(embeddings, clusters, cluster_owner):
    row_count = embeddings.shape[0]
    feature_width = embeddings.shape[1]
    groups_total = lax.axis_size("group")
    capacity = 3 * row_count // (2 * groups_total)
    slot_count = groups_total * capacity
    cluster_total = cluster_owner.shape[0]
    table_hit = clusters[:, None] == jnp.arange(cluster_total, dtype=jnp.int32)[None, :]
    group_of = jnp.sum(jnp.where(table_hit, cluster_owner[None, :], 0), axis=1)
    same_group = group_of[:, None] == group_of[None, :]
    row_index = jnp.arange(row_count, dtype=jnp.int32)
    earlier = row_index[None, :] < row_index[:, None]
    rank_in = jnp.sum(same_group & earlier, axis=1)
    slot_of = group_of * capacity + rank_in
    slot_index = jnp.arange(slot_count, dtype=jnp.int32)
    placing = slot_index[:, None] == slot_of[None, :]
    outgoing = jnp.dot(
        placing.astype(jnp.bfloat16), embeddings, preferred_element_type=jnp.float32
    ).astype(jnp.bfloat16)
    outgoing_ids = jnp.sum(jnp.where(placing, clusters[None, :] + 1, 0), axis=1) - 1
    arrived, arrived_ids = (
        lax.all_to_all(
            outgoing.reshape(groups_total, capacity, feature_width),
            "group",
            split_axis=0,
            concat_axis=0,
            tiled=True,
        ),
        lax.all_to_all(
            outgoing_ids.reshape(groups_total, capacity),
            "group",
            split_axis=0,
            concat_axis=0,
            tiled=True,
        ),
    )
    queries = arrived.reshape(slot_count, feature_width)
    query_ids = arrived_ids.reshape(slot_count)
    start_state = (
        jnp.zeros((slot_count,), jnp.float32),
        jnp.ones((slot_count,), jnp.float32),
        jnp.zeros((slot_count, feature_width), jnp.float32),
    )
    tile_pos = lax.axis_index("tile")
    query_pos = tile_pos * slot_count + jnp.arange(slot_count, dtype=jnp.int32)
    key_rows = lax.all_gather(queries, "tile", axis=0, tiled=True)
    key_ids = lax.all_gather(query_ids, "tile", axis=0, tiled=True)
    key_pos = jnp.arange(key_rows.shape[0], dtype=jnp.int32)
    scores = block_scores(queries, query_ids, key_rows, key_ids)
    usable = (key_ids[None, :] >= 0) & (key_pos[None, :] != query_pos[:, None])
    partials = combine_terms(start_state, partial_terms(scores, usable, key_rows))
    row_peak, row_total, weighted = partials
    lse_slots = row_peak + jnp.log(row_total)
    neighbour_slots = (weighted / row_total[:, None]).astype(jnp.bfloat16)
    back_rows, back_lse = (
        lax.all_to_all(
            neighbour_slots.reshape(groups_total, capacity, feature_width),
            "group",
            split_axis=0,
            concat_axis=0,
            tiled=True,
        ),
        lax.all_to_all(
            lse_slots.reshape(groups_total, capacity).astype(jnp.bfloat16),
            "group",
            split_axis=0,
            concat_axis=0,
            tiled=True,
        ).astype(jnp.float32),
    )
    flat_rows = back_rows.reshape(slot_count, feature_width)
    neighbours = jnp.take(flat_rows, slot_of, axis=0)
    log_mass = jnp.take(back_lse.reshape(slot_count), slot_of, axis=0).astype(jnp.float32)
    return (neighbours, log_mass)


def solution(mesh):
    placed = (P(("group", "tile"), None), P(("group", "tile")), P())
    return jax.shard_map(
        per_device,
        mesh=mesh,
        in_specs=placed,
        out_specs=(P(("group", "tile"), None), P(("group", "tile"))),
        check_vma=False,
    )
```

profile of v0, /device:TPU:1, one launch (start us, length us, event | category | flops | bytes accessed | tf_op | source)
XLA Modules:
  0.0 218.7 jit_solution(13662327656676615391)
XLA Ops:
  7.2 0.8 select_reduce_fusion.2
  8.3 0.7 multiply_add_fusion
  9.0 0.6 convolution_convert_fusion
  9.6 19.4 %all_to_all.22 = bf16[8,72,768]{2,1,0:T(8,128)(2,1)} all-to-all(bf16[8,72,768]{2,1,0:T(8,128)(2,1)S(1)} %bitcast.12), channel_id=1, replica_groups=mesh['group'=8,'tile'=16] {'group'}, dimensions={0} | all-to-all | bytes 1769472 | tf_op jit(solution)/shard_map/all_to_all | solution.py:58
  29.2 0.7 sub.55
  29.9 4.0 %all-to-all-start = ((s32[8,1,72]{2,1,0:T(1,128)}), s32[8,1,72]{2,1,0:T(1,128)S(1)}, u32[]{:S(2)}, u32[]{:S(2)}) async-start(s32[8,1,72]{2,1,0:T(1,128)} %sub.55), calls=%async_computation | async-start | bytes 8192 | tf_op jit(solution)/shard_map/all_to_all | solution.py:65
  33.9 1.2 dynamic-slice
  35.8 2.6 %all-to-all-done = s32[8,1,72]{2,1,0:T(1,128)S(1)} async-done(((s32[8,1,72]{2,1,0:T(1,128)}), s32[8,1,72]{2,1,0:T(1,128)S(1)}, u32[]{:S(2)}, u32[]{:S(2)}) %all-to-all-start) | async-done | bytes 2336 | tf_op jit(solution)/shard_map/all_to_all | solution.py:65
  38.4 0.5 broadcast.121
  38.9 0.7 reduce.9
  39.7 0.3 dynamic-update-slice
  40.0 63.1 %all-reduce = s32[9216]{0:T(1024)S(1)} all-reduce(s32[9216]{0:T(1024)S(1)} %dynamic-update-slice), channel_id=1, replica_groups=mesh['group'=8,'tile'=16] {'tile'}, use_global_device_ids=true, to_apply=%add | all-reduce | flops 9216 | bytes 73728
  103.1 25.9 %all-gather.2.cloned.1.call-done = bf16[9216,768]{1,0:T(8,128)(2,1)} async-done(((bf16[576,768]{1,0:T(8,128)(2,1)}), bf16[9216,768]{1,0:T(8,128)(2,1)}) %all-gather.2.cloned.1.call-update) | async-done | bytes 14155792 | tf_op jit(solution)/shard_map/all_gather | solution.py:82
  128.9 18.6 %select_reduce_fusion = (f32[576]{0:T(1024)S(1)}, f32[576,9216]{1,0:T(8,128)}) fusion(s32[9216]{0:T(1024)S(1)} %all-reduce, s32[576]{0:T(1024)S(1)} %iota_add_fusion, s32[576]{0:T(1024)S(1)} %reshape.184, pred[9216]{0:T(1024)(128)(4,1)S(1)} %broadcast_compare_fusion, bf16[576,768]{1,0:T(8,128)(2,1)} %bitcast.11, ...), kind=kOutput, calls=%fused_computation.3 | convolution fusion | flops 8196193792 | bytes 36327168 | tf_op jit(solution)/shard_map/dot_general | solution.py:13
  147.6 13.3 %fusion.17 = f32[576]{0:T(1024)S(1)} fusion(f32[576]{0:T(1024)S(1)} %get-tuple-element.6, s32[9216]{0:T(1024)S(1)} %all-reduce, s32[576]{0:T(1024)S(1)} %reshape.184, f32[576,9216]{1,0:T(8,128)} %get-tuple-element.7, s32[576]{0:T(1024)S(1)} %iota_add_fusion, pred[9216]{0:T(1024)(128)(4,1)S(1)} %broadcast_compare_fusion), kind=kLoop, calls=%fused_computation.46 | loop fusion | flops 47775168 | bytes 21288960 | tf_op jit(solution)/shard_map/reduce_sum | solution.py:23
  161.0 0.6 copy.5
  161.6 5.0 %all-to-all-start.3 = ((bf16[8,1,72]{2,1,0:T(2,128)(2,1)}), bf16[8,1,72]{2,1,0:T(2,128)(2,1)S(1)}, u32[]{:S(2)}, u32[]{:S(2)}) async-start(bf16[8,1,72]{2,1,0:T(2,128)(2,1)} %copy.5), calls=%async_computation.3 | async-start | bytes 8192 | tf_op jit(solution)/shard_map/all_to_all | solution.py:99
  166.6 24.0 %divide_convert_fusion = bf16[576,768]{1,0:T(8,128)(2,1)} fusion(bf16[9216,768]{1,0:T(8,128)(2,1)} %all-gather.2.cloned.1.call-done, f32[576]{0:T(1024)S(1)} %get-tuple-element.5, f32[576]{0:T(1024)S(1)} %get-tuple-element.4, f32[576,9216]{1,0:T(8,128)} %get-tuple-element.7, f32[576]{0:T(1024)S(1)} %get-tuple-element.6, s32[9216]{0:T(1024)S(1)} %all-reduce, ...), kind=kOutput, calls=%fused_computation.9 | convolution fusion | flops 8202829824 | bytes 36331776 | tf_op jit(solution)/shard_map/dot_general | solution.py:24
  190.6 4.8 %all-to-all-start.2 = ((bf16[8,72,768]{2,1,0:T(8,128)(2,1)}), bf16[8,72,768]{2,1,0:T(8,128)(2,1)S(1)}, u32[]{:S(2)}, u32[]{:S(2)}) async-start(bf16[8,72,768]{2,1,0:T(8,128)(2,1)} %bitcast.3), calls=%async_computation.2 | async-start | bytes 1769472 | tf_op jit(solution)/shard_map/all_to_all | solution.py:92
  195.5 1.9 gather_fusion.1
  197.4 0.6 broadcast_select_fusion.1
  198.0 10.7 %all-to-all-done.2 = bf16[8,72,768]{2,1,0:T(8,128)(2,1)S(1)} async-done(((bf16[8,72,768]{2,1,0:T(8,128)(2,1)}), bf16[8,72,768]{2,1,0:T(8,128)(2,1)S(1)}, u32[]{:S(2)}, u32[]{:S(2)}) %all-to-all-start.2) | async-done | bytes 884768 | tf_op jit(solution)/shard_map/all_to_all | solution.py:92
  208.8 2.2 gather_fusion
  210.9 0.9 broadcast_select_fusion
  (20 shorter events, 0.9 us)
Async XLA Ops:
  7.2 1.8 copy-start
  7.2 121.8 %all-gather.2.cloned.1.call-start = ((), (), s32[]{:S(2)}) async-start(), calls=%async_computation.4 | async-start | bytes 15040512 | tf_op jit(solution)/shard_map/all_gather | solution.py:82
  29.9 8.6 %all-to-all-start = ((s32[8,1,72]{2,1,0:T(1,128)}), s32[8,1,72]{2,1,0:T(1,128)S(1)}, u32[]{:S(2)}, u32[]{:S(2)}) async-start(s32[8,1,72]{2,1,0:T(1,128)} %sub.55), calls=%async_computation | async-start | bytes 8192 | tf_op jit(solution)/shard_map/all_to_all | solution.py:65
  161.6 29.0 %all-to-all-start.3 = ((bf16[8,1,72]{2,1,0:T(2,128)(2,1)}), bf16[8,1,72]{2,1,0:T(2,128)(2,1)S(1)}, u32[]{:S(2)}, u32[]{:S(2)}) async-start(bf16[8,1,72]{2,1,0:T(2,128)(2,1)} %copy.5), calls=%async_computation.3 | async-start | bytes 8192 | tf_op jit(solution)/shard_map/all_to_all | solution.py:99
  190.6 18.1 %all-to-all-start.2 = ((bf16[8,72,768]{2,1,0:T(8,128)(2,1)}), bf16[8,72,768]{2,1,0:T(8,128)(2,1)S(1)}, u32[]{:S(2)}, u32[]{:S(2)}) async-start(bf16[8,72,768]{2,1,0:T(8,128)(2,1)} %bitcast.3), calls=%async_computation.2 | async-start | bytes 1769472 | tf_op jit(solution)/shard_map/all_to_all | solution.py:92
Sparse Core Ops, SparseCore 0:
  29.1 99.7 all-gather.1
where the time goes:
time: 219 us
  blocking collectives  82.4 us (38%)
  matrix products  43.2 us (20%)
  waiting for transfers between devices  39.3 us (18%)
  other arithmetic  17.5 us (8%)
  between operations  14.8 us (7%)
  starting transfers between devices  13.8 us (6%)
  local copies, waits for them, and re-layouts  7.68 us (4%)
    unnamed x1, blocking collectives  63.1 us
    all_gather x1, waiting for transfers between devices, per_device(): key_rows = lax.all_gather(queries, 'tile', axis=0, tiled=True)  25.9 us
    dot_general x1, matrix products, partial_terms(): jnp.dot(weights.astype(jnp.bfloat16), key_rows, preferred_element_type=jn...  24 us
    all_to_all x1, blocking collectives, per_device(): lax.all_to_all(outgoing.reshape(groups_total, capacity, feature_width), '...  19.4 us
    dot_general x1, matrix products, block_scores(): lax.dot_general(queries, key_rows, (((1,), (1,)), ((), ())), preferred_el...  18.6 us
    reduce_sum x1, other arithmetic, partial_terms(): row_total = jnp.sum(weights, axis=1)  13.3 us
    all_to_all x1, waiting for transfers between devices, per_device(): lax.all_to_all(neighbour_slots.reshape(groups_total, capacity, feature_wi...  10.7 us
    all_to_all x1, starting transfers between devices, per_device(): lax.all_to_all(lse_slots.reshape(groups_total, capacity).astype(jnp.bfloa...  4.97 us
  transfers between devices with their start and end apart: 4, of which 3 were waited for; matrix products, arithmetic and copies ran while one was open for 14% of the time, Pallas kernels for 0%

commit v1 on v0

--- a/solution.py
+++ b/solution.py
@@ -35,6 +35,29 @@
 
 
 def per_device(embeddings, clusters, cluster_owner):
+
+    def domain_find(local, across):
+        v1 = lax.axis_size(across)
+        inter, val2, h_now = (v1, lax.axis_index(across), local.shape[0])
+        sheets = [h * inter if dev == 0 else h for dev, h in enumerate(local.shape)]
+        step_out = jnp.zeros(sheets, local.dtype)
+        x_next = parts_out = local
+        k_now = lax.dynamic_update_slice_in_dim(step_out, local, val2 * h_now, axis=0)
+        for t in range(1, inter // 2 + 1):
+            x_new = range(inter)
+            q_next = map(lambda dev: (dev, (dev + 1) % inter), x_new)
+            x_next = lax.ppermute(x_next, across, list(q_next))
+            k_now = lax.dynamic_update_slice_in_dim(
+                k_now, x_next, (val2 - t) % inter * h_now, axis=0
+            )
+            if 2 * t < inter:
+                side_arr = map(lambda dev: (dev, (dev - 1) % inter), range(inter))
+                parts_out = lax.ppermute(parts_out, across, list(side_arr))
+                k_now = lax.dynamic_update_slice_in_dim(
+                    k_now, parts_out, (val2 + t) % inter * h_now, axis=0
+                )
+        return k_now
+
     row_count = embeddings.shape[0]
     feature_width = embeddings.shape[1]
     groups_total = lax.axis_size("group")
@@ -79,7 +102,7 @@
     )
     tile_pos = lax.axis_index("tile")
     query_pos = tile_pos * slot_count + jnp.arange(slot_count, dtype=jnp.int32)
-    key_rows = lax.all_gather(queries, "tile", axis=0, tiled=True)
+    key_rows = domain_find(queries, "tile")
     key_ids = lax.all_gather(query_ids, "tile", axis=0, tiled=True)
     key_pos = jnp.arange(key_rows.shape[0], dtype=jnp.int32)
     scores = block_scores(queries, query_ids, key_rows, key_ids)

time: 219 us -> 358 us (1.63)
  waiting for transfers between devices: 39.3 us -> 117 us
  starting transfers between devices: 13.8 us -> 62.6 us
  local copies, waits for them, and re-layouts: 7.68 us -> 35.9 us
  between operations: 14.8 us -> 1.47 us
    ppermute x0 -> x15, waiting for transfers between devices: none -> 103 us  [the longest x8 101 us: domain_find(): x_next = lax.ppermute(x_next, across, list(q_next))]
    ppermute x0 -> x15, starting transfers between devices: none -> 29.2 us  [the longest x7 26.8 us: domain_find(): parts_out = lax.ppermute(parts_out, across, list(side_arr))]
    all_gather x1 -> x0, waiting for transfers between devices: 25.9 us -> none  [per_device(): key_rows = lax.all_gather(queries, 'tile', axis=0, tiled=True)]
    dynamic_update_slice x0 -> x16, local copies, waits for them, and re-layouts: none -> 20.6 us  [the longest x8 10.2 us: domain_find(): lax.dynamic_update_slice_in_dim(k_now, x_next, (val2 - t) % inter * h_now...]
    all_to_all x1, starting transfers between devices: 4.97 us -> 20.2 us  [per_device(): lax.all_to_all(lse_slots.reshape(groups_total, capacity).astype(jnp.bfloa...]
    broadcast_in_dim x0 -> x1, local copies, waits for them, and re-layouts: none -> 5.85 us  [domain_find(): step_out = jnp.zeros(sheets, local.dtype)]
    all_to_all x1, starting transfers between devices: 4.03 us -> 8.3 us  [per_device(): lax.all_to_all(outgoing_ids.reshape(groups_total, capacity), 'group', spl...]
  transfers between devices with their start and end apart: 4 -> 18, of which waited for: 3 -> 10; matrix products, arithmetic and copies ran while one was open for 14% -> 16% of each run, Pallas kernels for 0% -> 0%
where the time goes in v1:
time: 358 us; the launch traced here: 357 us
  waiting for transfers between devices  117 us (33%)
  blocking collectives  79.4 us (22%)
  starting transfers between devices  62.6 us (17%)
  matrix products  43.1 us (12%)
  local copies, waits for them, and re-layouts  35.9 us (10%)
  other arithmetic  17.5 us (5%)
    ppermute x8, waiting for transfers between devices, domain_find(): x_next = lax.ppermute(x_next, across, list(q_next))  101 us
    unnamed x1, blocking collectives  60.1 us
    ppermute x7, starting transfers between devices, domain_find(): parts_out = lax.ppermute(parts_out, across, list(side_arr))  26.8 us
    dot_general x1, matrix products, partial_terms(): jnp.dot(weights.astype(jnp.bfloat16), key_rows, preferred_element_type=jn...  24 us
    all_to_all x1, starting transfers between devices, per_device(): lax.all_to_all(lse_slots.reshape(groups_total, capacity).astype(jnp.bfloa...  20.2 us
    all_to_all x1, blocking collectives, per_device(): lax.all_to_all(outgoing.reshape(groups_total, capacity, feature_width), '...  19.3 us
    dot_general x1, matrix products, block_scores(): lax.dot_general(queries, key_rows, (((1,), (1,)), ((), ())), preferred_el...  18.6 us
    reduce_sum x1, other arithmetic, partial_terms(): row_total = jnp.sum(weights, axis=1)  13.3 us
  transfers between devices with their start and end apart: 18, of which 10 were waited for; matrix products, arithmetic and copies ran while one was open for 16% of the time, Pallas kernels for 0%

profile of v1, /device:TPU:1, one launch (start us, length us, event | category | flops | bytes accessed | tf_op | source)
XLA Modules:
  0.0 357.0 jit_solution(5180012194583866021)
XLA Ops:
  3.0 19.3 %all_to_all.22 = bf16[8,72,768]{2,1,0:T(8,128)(2,1)S(1)} all-to-all(bf16[8,72,768]{2,1,0:T(8,128)(2,1)S(1)} %bitcast.14), channel_id=1, replica_groups=mesh['group'=8,'tile'=16] {'group'}, dimensions={0} | all-to-all | bytes 1769472 | tf_op jit(solution)/shard_map/all_to_all | solution.py:81
  23.9 4.3 %collective-permute-start.1 = (bf16[576,768]{1,0:T(8,128)(2,1)S(1)}, bf16[576,768]{1,0:T(8,128)(2,1)S(1)}, u32[]{:S(2)}, u32[]{:S(2)}) collective-permute-start(bf16[576,768]{1,0:T(8,128)(2,1)S(1)} %bitcast.11), channel_id=1, source_target_pairs={{0,15},{1,0},{2,1},{3,2},{4,3},{5,4},{6,5},{7,6},{8,7},{9,8},{10,9... | collective-permute-start | bytes 2654216 | tf_op jit(solution)/shard_map/ppermute | solution.py:55
  28.2 19.2 %collective-permute-done = bf16[576,768]{1,0:T(8,128)(2,1)S(1)} collective-permute-done((bf16[576,768]{1,0:T(8,128)(2,1)S(1)}, bf16[576,768]{1,0:T(8,128)(2,1)S(1)}, u32[]{:S(2)}, u32[]{:S(2)}) %collective-permute-start) | collective-permute-done | bytes 884768 | tf_op jit(solution)/shard_map/ppermute | solution.py:49
  47.4 4.8 %collective-permute-start.3 = (bf16[576,768]{1,0:T(8,128)(2,1)S(1)}, bf16[576,768]{1,0:T(8,128)(2,1)S(1)}, u32[]{:S(2)}, u32[]{:S(2)}) collective-permute-start(bf16[576,768]{1,0:T(8,128)(2,1)S(1)} %collective-permute-done.1), channel_id=1, source_target_pairs={{0,15},{1,0},{2,1},{3,2},{4,3},{5,4},{6,5},{7,6},{8,7},{9,8},{10,9... | collective-permute-start | bytes 2654216 | tf_op jit(solution)/shard_map/ppermute | solution.py:55
  52.2 18.3 %collective-permute-done.2 = bf16[576,768]{1,0:T(8,128)(2,1)S(1)} collective-permute-done((bf16[576,768]{1,0:T(8,128)(2,1)S(1)}, bf16[576,768]{1,0:T(8,128)(2,1)S(1)}, u32[]{:S(2)}, u32[]{:S(2)}) %collective-permute-start.2) | collective-permute-done | bytes 884768 | tf_op jit(solution)/shard_map/ppermute | solution.py:49
  71.4 4.0 %collective-permute-start.5 = (bf16[576,768]{1,0:T(8,128)(2,1)S(1)}, bf16[576,768]{1,0:T(8,128)(2,1)S(1)}, u32[]{:S(2)}, u32[]{:S(2)}) collective-permute-start(bf16[576,768]{1,0:T(8,128)(2,1)S(1)} %collective-permute-done.3), channel_id=1, source_target_pairs={{0,15},{1,0},{2,1},{3,2},{4,3},{5,4},{6,5},{7,6},{8,7},{9,8},{10,9... | collective-permute-start | bytes 2654216 | tf_op jit(solution)/shard_map/ppermute | solution.py:55
  75.4 17.3 %collective-permute-done.4 = bf16[576,768]{1,0:T(8,128)(2,1)S(1)} collective-permute-done((bf16[576,768]{1,0:T(8,128)(2,1)S(1)}, bf16[576,768]{1,0:T(8,128)(2,1)S(1)}, u32[]{:S(2)}, u32[]{:S(2)}) %collective-permute-start.4) | collective-permute-done | bytes 884768 | tf_op jit(solution)/shard_map/ppermute | solution.py:49
  92.7 4.8 %collective-permute-start.7 = (bf16[576,768]{1,0:T(8,128)(2,1)S(1)}, bf16[576,768]{1,0:T(8,128)(2,1)}, u32[]{:S(2)}, u32[]{:S(2)}) collective-permute-start(bf16[576,768]{1,0:T(8,128)(2,1)S(1)} %collective-permute-done.5), channel_id=1, source_target_pairs={{0,15},{1,0},{2,1},{3,2},{4,3},{5,4},{6,5},{7,6},{8,7},{9,8},{10,9... | collective-permute-start | bytes 2654216 | tf_op jit(solution)/shard_map/ppermute | solution.py:55
  97.4 16.4 %collective-permute-done.6 = bf16[576,768]{1,0:T(8,128)(2,1)S(1)} collective-permute-done((bf16[576,768]{1,0:T(8,128)(2,1)S(1)}, bf16[576,768]{1,0:T(8,128)(2,1)S(1)}, u32[]{:S(2)}, u32[]{:S(2)}) %collective-permute-start.6) | collective-permute-done | bytes 884768 | tf_op jit(solution)/shard_map/ppermute | solution.py:49
  114.8 4.8 %collective-permute-start.9 = (bf16[576,768]{1,0:T(8,128)(2,1)}, bf16[576,768]{1,0:T(8,128)(2,1)}, u32[]{:S(2)}, u32[]{:S(2)}) collective-permute-start(bf16[576,768]{1,0:T(8,128)(2,1)} %collective-permute-done.7), channel_id=1, source_target_pairs={{0,15},{1,0},{2,1},{3,2},{4,3},{5,4},{6,5},{7,6},{8,7},{9,8},{10,9... | collective-permute-start | bytes 2654216 | tf_op jit(solution)/shard_map/ppermute | solution.py:55
  119.8 15.4 %collective-permute-done.8 = bf16[576,768]{1,0:T(8,128)(2,1)} collective-permute-done((bf16[576,768]{1,0:T(8,128)(2,1)S(1)}, bf16[576,768]{1,0:T(8,128)(2,1)}, u32[]{:S(2)}, u32[]{:S(2)}) %collective-permute-start.8) | collective-permute-done | bytes 884768 | tf_op jit(solution)/shard_map/ppermute | solution.py:49
  135.9 8.3 %all-to-all-start = ((s32[8,1,72]{2,1,0:T(1,128)}), s32[8,1,72]{2,1,0:T(1,128)S(1)}, u32[]{:S(2)}, u32[]{:S(2)}) async-start(s32[8,1,72]{2,1,0:T(1,128)} %sub.79), calls=%async_computation | async-start | bytes 8192 | tf_op jit(solution)/shard_map/all_to_all | solution.py:88
  146.1 3.0 all-to-all-done
  150.7 60.1 %all-reduce = s32[9216]{0:T(1024)S(1)} all-reduce(s32[9216]{0:T(1024)S(1)} %dynamic-update-slice), channel_id=1, replica_groups=mesh['group'=8,'tile'=16] {'tile'}, use_global_device_ids=true, to_apply=%add | all-reduce | flops 9216 | bytes 73728
  210.9 5.9 %broadcast_in_dim.75 = bf16[9216,768]{1,0:T(8,128)(2,1)} broadcast(bf16[]{:T(256)} %constant.131.clone.1), dimensions={} | broadcast | bytes 14155778 | tf_op jit(solution)/shard_map/broadcast_in_dim | solution.py:43
  224.4 4.1 %collective-permute-start.13 = (bf16[576,768]{1,0:T(8,128)(2,1)S(1)}, bf16[576,768]{1,0:T(8,128)(2,1)S(1)}, u32[]{:S(2)}, u32[]{:S(2)}) collective-permute-start(bf16[576,768]{1,0:T(8,128)(2,1)S(1)} %collective-permute-done.11), channel_id=1, source_target_pairs={{0,15},{1,0},{2,1},{3,2},{4,3},{5,4},{6,5},{7,6},{8,7},{9,8},{10,9... | collective-permute-start | bytes 2654216 | tf_op jit(solution)/shard_map/ppermute | solution.py:55
  229.5 3.7 %collective-permute-done.12 = bf16[576,768]{1,0:T(8,128)(2,1)S(1)} collective-permute-done((bf16[576,768]{1,0:T(8,128)(2,1)}, bf16[576,768]{1,0:T(8,128)(2,1)S(1)}, u32[]{:S(2)}, u32[]{:S(2)}) %collective-permute-start.12) | collective-permute-done | bytes 884768 | tf_op jit(solution)/shard_map/ppermute | solution.py:49
  246.8 11.1 %collective-permute-done.14 = bf16[576,768]{1,0:T(8,128)(2,1)S(1)} collective-permute-done((bf16[576,768]{1,0:T(8,128)(2,1)S(1)}, bf16[576,768]{1,0:T(8,128)(2,1)S(1)}, u32[]{:S(2)}, u32[]{:S(2)}) %collective-permute-start.14) | collective-permute-done | bytes 884768 | tf_op jit(solution)/shard_map/ppermute | solution.py:49
  258.9 18.6 %select_reduce_fusion = (f32[576]{0:T(1024)S(1)}, f32[576,9216]{1,0:T(8,128)}) fusion(s32[9216]{0:T(1024)S(1)} %all-reduce, s32[576]{0:T(1024)S(1)} %iota_add_fusion, s32[576]{0:T(1024)S(1)} %reshape.184, pred[9216]{0:T(1024)(128)(4,1)S(1)} %broadcast_compare_fusion, bf16[576,768]{1,0:T(8,128)(2,1)S(1)} %bitcast.13, ...), kind=kOutput, calls=%fused_computation.3 | convolution fusion | flops 8196193792 | bytes 36327168 | tf_op jit(solution)/shard_map/dot_general | solution.py:13
  277.4 13.3 %fusion.17 = f32[576]{0:T(1024)S(1)} fusion(f32[576]{0:T(1024)S(1)} %get-tuple-element.6, s32[9216]{0:T(1024)S(1)} %all-reduce, s32[576]{0:T(1024)S(1)} %reshape.184, f32[576,9216]{1,0:T(8,128)} %get-tuple-element.7, s32[576]{0:T(1024)S(1)} %iota_add_fusion, pred[9216]{0:T(1024)(128)(4,1)S(1)} %broadcast_compare_fusion), kind=kLoop, calls=%fused_computation.62 | loop fusion | flops 47775168 | bytes 21288960 | tf_op jit(solution)/shard_map/reduce_sum | solution.py:23
  291.5 20.2 %all-to-all-start.3 = ((bf16[8,1,72]{2,1,0:T(2,128)(2,1)}), bf16[8,1,72]{2,1,0:T(2,128)(2,1)S(1)}, u32[]{:S(2)}, u32[]{:S(2)}) async-start(bf16[8,1,72]{2,1,0:T(2,128)(2,1)} %copy.5), calls=%async_computation.3 | async-start | bytes 8192 | tf_op jit(solution)/shard_map/all_to_all | solution.py:122
  311.8 24.0 %divide_convert_fusion = bf16[576,768]{1,0:T(8,128)(2,1)} fusion(bf16[9216,768]{1,0:T(8,128)(2,1)} %constant_dynamic-update-slice_fusion, f32[576]{0:T(1024)S(1)} %get-tuple-element.5, f32[576]{0:T(1024)S(1)} %get-tuple-element.4, f32[576,9216]{1,0:T(8,128)} %get-tuple-element.7, f32[576]{0:T(1024)S(1)} %get-tuple-element.6, s32[9216]{0:T(1024)S(1)} %all-reduce, ...), kind=kOutput, calls=%fused_computation.9 | convolution fusion | flops 8202829824 | bytes 36331776 | tf_op jit(solution)/shard_map/dot_general | solution.py:24
  335.7 4.8 %all-to-all-start.2 = ((bf16[8,72,768]{2,1,0:T(8,128)(2,1)}), bf16[8,72,768]{2,1,0:T(8,128)(2,1)S(1)}, u32[]{:S(2)}, u32[]{:S(2)}) async-start(bf16[8,72,768]{2,1,0:T(8,128)(2,1)} %bitcast.3), calls=%async_computation.2 | async-start | bytes 1769472 | tf_op jit(solution)/shard_map/all_to_all | solution.py:115
  343.2 10.7 %all-to-all-done.2 = bf16[8,72,768]{2,1,0:T(8,128)(2,1)S(1)} async-done(((bf16[8,72,768]{2,1,0:T(8,128)(2,1)}), bf16[8,72,768]{2,1,0:T(8,128)(2,1)S(1)}, u32[]{:S(2)}, u32[]{:S(2)}) %all-to-all-start.2) | async-done | bytes 884768 | tf_op jit(solution)/shard_map/all_to_all | solution.py:115
  (84 shorter events, 39.3 us)
Async XLA Ops:
  22.3 25.2 %collective-permute-start = (bf16[576,768]{1,0:T(8,128)(2,1)S(1)}, bf16[576,768]{1,0:T(8,128)(2,1)S(1)}, u32[]{:S(2)}, u32[]{:S(2)}) collective-permute-start(bf16[576,768]{1,0:T(8,128)(2,1)S(1)} %bitcast.10), channel_id=1, source_target_pairs={{0,1},{1,2},{2,3},{3,4},{4,5},{5,6},{6,7},{7,8},{8,9},{9,10},{10,1... | collective-permute-start | bytes 2654216 | tf_op jit(solution)/shard_map/ppermute | solution.py:49
  23.9 23.5 %collective-permute-start.1 = (bf16[576,768]{1,0:T(8,128)(2,1)S(1)}, bf16[576,768]{1,0:T(8,128)(2,1)S(1)}, u32[]{:S(2)}, u32[]{:S(2)}) collective-permute-start(bf16[576,768]{1,0:T(8,128)(2,1)S(1)} %bitcast.11), channel_id=1, source_target_pairs={{0,15},{1,0},{2,1},{3,2},{4,3},{5,4},{6,5},{7,6},{8,7},{9,8},{10,9... | collective-permute-start | bytes 2654216 | tf_op jit(solution)/shard_map/ppermute | solution.py:55
  47.4 23.1 %collective-permute-start.2 = (bf16[576,768]{1,0:T(8,128)(2,1)S(1)}, bf16[576,768]{1,0:T(8,128)(2,1)S(1)}, u32[]{:S(2)}, u32[]{:S(2)}) collective-permute-start(bf16[576,768]{1,0:T(8,128)(2,1)S(1)} %collective-permute-done), channel_id=1, source_target_pairs={{0,1},{1,2},{2,3},{3,4},{4,5},{5,6},{6,7},{7,8},{8,9},{9,10},{10,1... | collective-permute-start | bytes 2654216 | tf_op jit(solution)/shard_map/ppermute | solution.py:49
  47.4 23.1 %collective-permute-start.3 = (bf16[576,768]{1,0:T(8,128)(2,1)S(1)}, bf16[576,768]{1,0:T(8,128)(2,1)S(1)}, u32[]{:S(2)}, u32[]{:S(2)}) collective-permute-start(bf16[576,768]{1,0:T(8,128)(2,1)S(1)} %collective-permute-done.1), channel_id=1, source_target_pairs={{0,15},{1,0},{2,1},{3,2},{4,3},{5,4},{6,5},{7,6},{8,7},{9,8},{10,9... | collective-permute-start | bytes 2654216 | tf_op jit(solution)/shard_map/ppermute | solution.py:55
  70.5 22.1 %collective-permute-start.4 = (bf16[576,768]{1,0:T(8,128)(2,1)S(1)}, bf16[576,768]{1,0:T(8,128)(2,1)S(1)}, u32[]{:S(2)}, u32[]{:S(2)}) collective-permute-start(bf16[576,768]{1,0:T(8,128)(2,1)S(1)} %collective-permute-done.2), channel_id=1, source_target_pairs={{0,1},{1,2},{2,3},{3,4},{4,5},{5,6},{6,7},{7,8},{8,9},{9,10},{10,1... | collective-permute-start | bytes 2654216 | tf_op jit(solution)/shard_map/ppermute | solution.py:49
  71.4 21.2 %copy-start.3 = (bf16[576,768]{1,0:T(8,128)(2,1)}, bf16[576,768]{1,0:T(8,128)(2,1)S(1)}, u32[]{:S(2)}) copy-start(bf16[576,768]{1,0:T(8,128)(2,1)S(1)} %collective-permute-done.3) | copy-start | bytes 2654212
  71.4 21.2 %collective-permute-start.5 = (bf16[576,768]{1,0:T(8,128)(2,1)S(1)}, bf16[576,768]{1,0:T(8,128)(2,1)S(1)}, u32[]{:S(2)}, u32[]{:S(2)}) collective-permute-start(bf16[576,768]{1,0:T(8,128)(2,1)S(1)} %collective-permute-done.3), channel_id=1, source_target_pairs={{0,15},{1,0},{2,1},{3,2},{4,3},{5,4},{6,5},{7,6},{8,7},{9,8},{10,9... | collective-permute-start | bytes 2654216 | tf_op jit(solution)/shard_map/ppermute | solution.py:55
  92.6 22.1 %copy-start.7 = (bf16[576,768]{1,0:T(8,128)(2,1)}, bf16[576,768]{1,0:T(8,128)(2,1)S(1)}, u32[]{:S(2)}) copy-start(bf16[576,768]{1,0:T(8,128)(2,1)S(1)} %collective-permute-done.4) | copy-start | bytes 2654212
  92.6 21.2 %collective-permute-start.6 = (bf16[576,768]{1,0:T(8,128)(2,1)S(1)}, bf16[576,768]{1,0:T(8,128)(2,1)S(1)}, u32[]{:S(2)}, u32[]{:S(2)}) collective-permute-start(bf16[576,768]{1,0:T(8,128)(2,1)S(1)} %collective-permute-done.4), channel_id=1, source_target_pairs={{0,1},{1,2},{2,3},{3,4},{4,5},{5,6},{6,7},{7,8},{8,9},{9,10},{10,1... | collective-permute-start | bytes 2654216 | tf_op jit(solution)/shard_map/ppermute | solution.py:49
  92.7 22.1 %copy-start.9 = (bf16[576,768]{1,0:T(8,128)(2,1)}, bf16[576,768]{1,0:T(8,128)(2,1)S(1)}, u32[]{:S(2)}) copy-start(bf16[576,768]{1,0:T(8,128)(2,1)S(1)} %collective-permute-done.5) | copy-start | bytes 2654212
  92.7 22.1 %collective-permute-start.7 = (bf16[576,768]{1,0:T(8,128)(2,1)S(1)}, bf16[576,768]{1,0:T(8,128)(2,1)}, u32[]{:S(2)}, u32[]{:S(2)}) collective-permute-start(bf16[576,768]{1,0:T(8,128)(2,1)S(1)} %collective-permute-done.5), channel_id=1, source_target_pairs={{0,15},{1,0},{2,1},{3,2},{4,3},{5,4},{6,5},{7,6},{8,7},{9,8},{10,9... | collective-permute-start | bytes 2654216 | tf_op jit(solution)/shard_map/ppermute | solution.py:55
  114.8 20.4 %collective-permute-start.8 = (bf16[576,768]{1,0:T(8,128)(2,1)S(1)}, bf16[576,768]{1,0:T(8,128)(2,1)}, u32[]{:S(2)}, u32[]{:S(2)}) collective-permute-start(bf16[576,768]{1,0:T(8,128)(2,1)S(1)} %collective-permute-done.6), channel_id=1, source_target_pairs={{0,1},{1,2},{2,3},{3,4},{4,5},{5,6},{6,7},{7,8},{8,9},{9,10},{10,1... | collective-permute-start | bytes 2654216 | tf_op jit(solution)/shard_map/ppermute | solution.py:49
  114.8 96.0 %collective-permute-start.9 = (bf16[576,768]{1,0:T(8,128)(2,1)}, bf16[576,768]{1,0:T(8,128)(2,1)}, u32[]{:S(2)}, u32[]{:S(2)}) collective-permute-start(bf16[576,768]{1,0:T(8,128)(2,1)} %collective-permute-done.7), channel_id=1, source_target_pairs={{0,15},{1,0},{2,1},{3,2},{4,3},{5,4},{6,5},{7,6},{8,7},{9,8},{10,9... | collective-permute-start | bytes 2654216 | tf_op jit(solution)/shard_map/ppermute | solution.py:55
  135.2 82.6 %collective-permute-start.10 = (bf16[576,768]{1,0:T(8,128)(2,1)}, bf16[576,768]{1,0:T(8,128)(2,1)}, u32[]{:S(2)}, u32[]{:S(2)}) collective-permute-start(bf16[576,768]{1,0:T(8,128)(2,1)} %collective-permute-done.8), channel_id=1, source_target_pairs={{0,1},{1,2},{2,3},{3,4},{4,5},{5,6},{6,7},{7,8},{8,9},{9,10},{10,1... | collective-permute-start | bytes 2654216 | tf_op jit(solution)/shard_map/ppermute | solution.py:49
  135.9 13.2 %all-to-all-start = ((s32[8,1,72]{2,1,0:T(1,128)}), s32[8,1,72]{2,1,0:T(1,128)S(1)}, u32[]{:S(2)}, u32[]{:S(2)}) async-start(s32[8,1,72]{2,1,0:T(1,128)} %sub.79), calls=%async_computation | async-start | bytes 8192 | tf_op jit(solution)/shard_map/all_to_all | solution.py:88
  210.8 11.7 %copy-start.8 = (bf16[576,768]{1,0:T(8,128)(2,1)S(1)}, bf16[576,768]{1,0:T(8,128)(2,1)}, u32[]{:S(2)}) copy-start(bf16[576,768]{1,0:T(8,128)(2,1)} %copy-done.7) | copy-start | bytes 2654212
  210.8 12.6 %copy-start.10 = (bf16[576,768]{1,0:T(8,128)(2,1)S(1)}, bf16[576,768]{1,0:T(8,128)(2,1)}, u32[]{:S(2)}) copy-start(bf16[576,768]{1,0:T(8,128)(2,1)} %copy-done.9) | copy-start | bytes 2654212
  210.8 17.7 %copy-start.6 = (bf16[576,768]{1,0:T(8,128)(2,1)S(1)}, bf16[576,768]{1,0:T(8,128)(2,1)}, u32[]{:S(2)}) copy-start(bf16[576,768]{1,0:T(8,128)(2,1)} %copy-done.5) | copy-start | bytes 2654212
  210.8 13.6 %collective-permute-start.11 = (bf16[576,768]{1,0:T(8,128)(2,1)}, bf16[576,768]{1,0:T(8,128)(2,1)S(1)}, u32[]{:S(2)}, u32[]{:S(2)}) collective-permute-start(bf16[576,768]{1,0:T(8,128)(2,1)} %collective-permute-done.9), channel_id=1, source_target_pairs={{0,15},{1,0},{2,1},{3,2},{4,3},{5,4},{6,5},{7,6},{8,7},{9,8},{10,9... | collective-permute-start | bytes 2654216 | tf_op jit(solution)/shard_map/ppermute | solution.py:55
  217.7 15.5 %collective-permute-start.12 = (bf16[576,768]{1,0:T(8,128)(2,1)}, bf16[576,768]{1,0:T(8,128)(2,1)S(1)}, u32[]{:S(2)}, u32[]{:S(2)}) collective-permute-start(bf16[576,768]{1,0:T(8,128)(2,1)} %collective-permute-done.10), channel_id=1, source_target_pairs={{0,1},{1,2},{2,3},{3,4},{4,5},{5,6},{6,7},{7,8},{8,9},{9,10},{10,1... | collective-permute-start | bytes 2654216 | tf_op jit(solution)/shard_map/ppermute | solution.py:49
  224.4 21.4 %collective-permute-start.13 = (bf16[576,768]{1,0:T(8,128)(2,1)S(1)}, bf16[576,768]{1,0:T(8,128)(2,1)S(1)}, u32[]{:S(2)}, u32[]{:S(2)}) collective-permute-start(bf16[576,768]{1,0:T(8,128)(2,1)S(1)} %collective-permute-done.11), channel_id=1, source_target_pairs={{0,15},{1,0},{2,1},{3,2},{4,3},{5,4},{6,5},{7,6},{8,7},{9,8},{10,9... | collective-permute-start | bytes 2654216 | tf_op jit(solution)/shard_map/ppermute | solution.py:55
  233.2 24.7 %collective-permute-start.14 = (bf16[576,768]{1,0:T(8,128)(2,1)S(1)}, bf16[576,768]{1,0:T(8,128)(2,1)S(1)}, u32[]{:S(2)}, u32[]{:S(2)}) collective-permute-start(bf16[576,768]{1,0:T(8,128)(2,1)S(1)} %collective-permute-done.12), channel_id=1, source_target_pairs={{0,1},{1,2},{2,3},{3,4},{4,5},{5,6},{6,7},{7,8},{8,9},{9,10},{10,1... | collective-permute-start | bytes 2654216 | tf_op jit(solution)/shard_map/ppermute | solution.py:49
  291.5 44.2 %all-to-all-start.3 = ((bf16[8,1,72]{2,1,0:T(2,128)(2,1)}), bf16[8,1,72]{2,1,0:T(2,128)(2,1)S(1)}, u32[]{:S(2)}, u32[]{:S(2)}) async-start(bf16[8,1,72]{2,1,0:T(2,128)(2,1)} %copy.5), calls=%async_computation.3 | async-start | bytes 8192 | tf_op jit(solution)/shard_map/all_to_all | solution.py:122
  335.7 18.2 %all-to-all-start.2 = ((bf16[8,72,768]{2,1,0:T(8,128)(2,1)}), bf16[8,72,768]{2,1,0:T(8,128)(2,1)S(1)}, u32[]{:S(2)}, u32[]{:S(2)}) async-start(bf16[8,72,768]{2,1,0:T(8,128)(2,1)} %bitcast.3), calls=%async_computation.2 | async-start | bytes 1769472 | tf_op jit(solution)/shard_map/all_to_all | solution.py:115
  (5 other events, 24.0 us)
